TPU v7x, 32 devices: a whole 2x2x4 slice. The times are simulated.
32 devices in a mesh: dp: 8 (over y, x, core), seq: 4 (over z).
Axes of the slice: x: 2, y: 2, z: 4, core: 2. Of those that a mesh axis runs over, the one named last changes fastest.
Arguments:
- hidden_in: bfloat16 [8, 2048, 2048], P('dp', 'seq'), may hold values from -6 to 6
- memory: bfloat16 [8, 2048, 2048], P('dp', 'seq'), may hold values from -6 to 6
- segments: int32 [8, 2048], P('dp'), may hold values from 0 to 3, never falling along the last dimension, each value on 1 to 1200 neighbouring positions
- gain_attn: bfloat16 [2048], P(('dp', 'seq')), may hold values from 0.25 to 1.75
- w_query: bfloat16 [2048, 2048], P(('dp', 'seq')), may hold values from -0.125 to 0.125
- w_key: bfloat16 [2048, 2048], P(('dp', 'seq')), may hold values from -0.125 to 0.125
- w_value: bfloat16 [2048, 2048], P(('dp', 'seq')), may hold values from -0.125 to 0.125
- w_out: bfloat16 [2048, 2048], P(('dp', 'seq')), may hold values from -0.75 to 0.75
- gain_ffn: bfloat16 [2048], P(('dp', 'seq')), may hold values from 0.25 to 1.75
- w_gate: bfloat16 [5504, 2048], P(('dp', 'seq')), may hold values from -0.125 to 0.125
- w_up: bfloat16 [5504, 2048], P(('dp', 'seq')), may hold values from -0.125 to 0.125
- w_down: bfloat16 [5504, 2048], P(('dp', 'seq')), may hold values from -0.078125 to 0.078125
- cotangent: bfloat16 [8, 2048, 2048], P('dp', 'seq'), may hold values from -6 to 6
Outputs:
- layer_out: bfloat16 [8, 2048, 2048], P('dp', 'seq')
- grad_hidden: float32 [8, 2048, 2048], P('dp', 'seq')
- grad_memory: float32 [8, 2048, 2048], P('dp', 'seq')
- grad_gain_attn: float32 [2048], P(('dp', 'seq'))
- grad_w_query: float32 [2048, 2048], P(('dp', 'seq'))
- grad_w_key: float32 [2048, 2048], P(('dp', 'seq'))
- grad_w_value: float32 [2048, 2048], P(('dp', 'seq'))
- grad_w_out: float32 [2048, 2048], P(('dp', 'seq'))
- grad_gain_ffn: float32 [2048], P(('dp', 'seq'))
- grad_w_gate: float32 [5504, 2048], P(('dp', 'seq'))
- grad_w_up: float32 [5504, 2048], P(('dp', 'seq'))
- grad_w_down: float32 [5504, 2048], P(('dp', 'seq'))
Inputs may be any that keep to these rules, and one draw needn't show every extreme that they name: `segments`: along each sequence the numbers never fall; each number is held by 1 to 1200 consecutive tokens, and in every draw some document has exactly 1200.
All inputs are finite; a program needn't handle non-finite values.
Results may differ from a plain program's by a relative error of at most 0.019.
Values may be sent and summed in bfloat16 or wider, within the bound.
A program may use at most 384 MiB of HBM per device.

v0:
```python
import jax
import jax.numpy as jnp
from jax import lax
from jax.sharding import PartitionSpec as P

HEAD_DIM = 128
EPSILON = 1e-06
MASKED = -1e30


def rms_scale(values):
    return lax.rsqrt(jnp.mean(values * values, axis=-1, keepdims=True) + EPSILON)


def norm_back(grad_normed, normed, rstd, gain):
    scaled = grad_normed * gain
    return rstd * (scaled - normed * jnp.mean(scaled * normed, axis=-1, keepdims=True))


def visible(segment_ids, start, rows):
    length = segment_ids.shape[0]
    query_pos = start + lax.broadcasted_iota(jnp.int32, (rows, length), 0)
    key_pos = lax.broadcasted_iota(jnp.int32, (rows, length), 1)
    query_segment = lax.dynamic_slice_in_dim(segment_ids, start, rows)
    return (key_pos <= query_pos) & (query_segment[:, None] == segment_ids[None, :])


def block_scores(query_block, keys, segment_ids, start):
    rows = query_block.shape[0]
    scale = query_block.shape[2] ** (-0.5)
    score = (
        jnp.einsum("qhd,khd->hqk", query_block, keys, preferred_element_type=jnp.float32) * scale
    )
    return jnp.where(visible(segment_ids, start, rows)[None], score, MASKED)


def attend_forward(query, key, value, segment_ids):
    length, heads, width = query.shape
    rows = min(512, length)

    def one_block(index):
        start = index * rows
        query_block = lax.dynamic_slice_in_dim(query, start, rows, 0)
        score = block_scores(query_block, key, segment_ids, start)
        top = jnp.max(score, axis=-1, keepdims=True)
        raised = jnp.exp(score - top)
        total = jnp.sum(raised, axis=-1, keepdims=True)
        prob_low = (raised / total).astype(jnp.bfloat16)
        context = jnp.einsum("hqk,khd->qhd", prob_low, value, preferred_element_type=jnp.float32)
        return (context.astype(jnp.bfloat16), (top + jnp.log(total))[..., 0])

    context, logsum = lax.map(one_block, jnp.arange(length // rows, dtype=jnp.int32))
    return (context.reshape(length, heads * width), logsum)


def attend_backward(query, key, value, segment_ids, logsum, grad_context):
    length, heads, width = query.shape
    rows = min(512, length)
    scale = width ** (-0.5)

    def one_block(carry, index):
        grad_key, grad_value = carry
        start = index * rows
        query_block = lax.dynamic_slice_in_dim(query, start, rows, 0)
        grad_block = lax.dynamic_slice_in_dim(grad_context, start, rows, 0)
        score = block_scores(query_block, key, segment_ids, start)
        prob = jnp.exp(score - logsum[index][..., None])
        grad_value = grad_value + jnp.einsum(
            "hqk,qhd->khd",
            prob.astype(jnp.bfloat16),
            grad_block,
            preferred_element_type=jnp.float32,
        )
        grad_prob = jnp.einsum(
            "qhd,khd->hqk", grad_block, value, preferred_element_type=jnp.float32
        )
        grad_score = (
            prob * (grad_prob - jnp.sum(prob * grad_prob, axis=-1, keepdims=True))
        ).astype(jnp.bfloat16)
        grad_query = (
            jnp.einsum("hqk,khd->qhd", grad_score, key, preferred_element_type=jnp.float32) * scale
        )
        grad_key = (
            grad_key
            + jnp.einsum(
                "hqk,qhd->khd", grad_score, query_block, preferred_element_type=jnp.float32
            )
            * scale
        )
        return ((grad_key, grad_value), grad_query.astype(jnp.bfloat16))

    zeros = jnp.zeros((length, heads, width), jnp.float32)
    (grad_key, grad_value), grad_query = lax.scan(
        one_block, (zeros, zeros), jnp.arange(length // rows, dtype=jnp.int32)
    )
    flat = (length, heads * width)
    return (
        grad_query.reshape(flat),
        grad_key.astype(jnp.bfloat16).reshape(flat),
        grad_value.astype(jnp.bfloat16).reshape(flat),
    )


def row_terms(left, right, blocks, share):
    term = jnp.einsum("tk,td->kd", left, right, preferred_element_type=jnp.float32)
    return term.reshape(blocks, share, right.shape[1])


def gain_terms(vector, blocks):
    return jnp.broadcast_to(vector[None, None, :], (blocks, 1, vector.shape[0]))


def shards(
    hidden_in,
    memory,
    segments,
    gain_attn,
    w_query,
    w_key,
    w_value,
    w_out,
    gain_ffn,
    w_gate,
    w_up,
    w_down,
    cotangent,
):
    seqs, piece, width = hidden_in.shape
    groups = lax.axis_size("seq")
    dp_count = lax.axis_size("dp")
    length = piece * groups
    heads_here = width // groups // HEAD_DIM
    count = seqs * piece
    share_d = w_query.shape[0]
    share_f = w_gate.shape[0]
    tokens = hidden_in.reshape(count, width)
    memory_flat = memory.reshape(count, width)
    grad_out = cotangent.reshape(count, width)
    hidden32 = tokens.astype(jnp.float32)
    rstd_in = rms_scale(hidden32)
    normed_in = hidden32 * rstd_in
    gain_piece = lax.all_gather(gain_attn, ("dp", "seq"), axis=0, tiled=True)
    query_rows = lax.all_gather(w_query, ("dp", "seq"), axis=0, tiled=True)
    key_rows = lax.all_gather(w_key, ("dp", "seq"), axis=0, tiled=True)
    value_rows = lax.all_gather(w_value, ("dp", "seq"), axis=0, tiled=True)
    gain32 = gain_piece.astype(jnp.float32)
    columns = (normed_in * gain32).astype(jnp.bfloat16)
    query = jnp.dot(columns, query_rows, preferred_element_type=jnp.float32)
    key = jnp.dot(memory_flat, key_rows, preferred_element_type=jnp.float32)
    value = jnp.dot(memory_flat, value_rows, preferred_element_type=jnp.float32)
    attn_in = columns
    query, key, value, attn_in, gain_attn_full = (query, key, value, attn_in, gain32)
    cube = (seqs, piece, width)
    query_heads, key_heads, value_heads = (
        lax.all_to_all(
            query.astype(jnp.bfloat16).reshape(cube), "seq", split_axis=2, concat_axis=1, tiled=True
        ),
        lax.all_to_all(
            key.astype(jnp.bfloat16).reshape(cube), "seq", split_axis=2, concat_axis=1, tiled=True
        ),
        lax.all_to_all(
            value.astype(jnp.bfloat16).reshape(cube), "seq", split_axis=2, concat_axis=1, tiled=True
        ),
    )
    head_shape = (length, heads_here, HEAD_DIM)

    def forward_one(item):
        query_seq, key_seq, value_seq, segment_ids = item
        return attend_forward(
            query_seq.reshape(head_shape),
            key_seq.reshape(head_shape),
            value_seq.reshape(head_shape),
            segment_ids,
        )

    context_heads, logsum = lax.map(forward_one, (query_heads, key_heads, value_heads, segments))
    context = lax.all_to_all(context_heads, "seq", split_axis=1, concat_axis=2, tiled=True).reshape(
        count, width
    )
    out_full, gain_ffn_full = (
        lax.all_gather(w_out, ("dp", "seq"), axis=0, tiled=True),
        lax.all_gather(gain_ffn, ("dp", "seq"), axis=0, tiled=True),
    )
    mid = hidden32 + jnp.dot(context, out_full, preferred_element_type=jnp.float32)
    rstd_mid = rms_scale(mid)
    normed_mid = mid * rstd_mid
    gain_ffn32 = gain_ffn_full.astype(jnp.float32)
    ffn_in = (normed_mid * gain_ffn32).astype(jnp.bfloat16)
    gate_rows, up_rows = lax.all_gather((w_gate, w_up), ("dp", "seq"), axis=0, tiled=True)
    gate_part = jnp.einsum("td,fd->tf", ffn_in, gate_rows, preferred_element_type=jnp.float32)
    up_part = jnp.einsum("td,fd->tf", ffn_in, up_rows, preferred_element_type=jnp.float32)
    both = jnp.stack((gate_part, up_part))
    gate = both[0]
    up = both[1]
    gate_sigmoid = jax.nn.sigmoid(gate)
    act = (gate * gate_sigmoid * up).astype(jnp.bfloat16)
    columns = act
    branch = jnp.dot(
        columns,
        lax.all_gather(w_down, ("dp", "seq"), axis=0, tiled=True),
        preferred_element_type=jnp.float32,
    )
    layer_out = (mid + branch).astype(jnp.bfloat16).reshape(cube)
    grad_act = jnp.einsum(
        "td,fd->tf",
        grad_out,
        lax.all_gather(w_down, ("dp", "seq"), axis=0, tiled=True),
        preferred_element_type=jnp.float32,
    )
    grad_gate = (grad_act * up * gate_sigmoid * (1.0 + gate * (1.0 - gate_sigmoid))).astype(
        jnp.bfloat16
    )
    grad_up = (grad_act * gate * gate_sigmoid).astype(jnp.bfloat16)
    gate_rows = lax.all_gather(w_gate, ("dp", "seq"), axis=0, tiled=True)
    up_rows = lax.all_gather(w_up, ("dp", "seq"), axis=0, tiled=True)
    total = jnp.dot(grad_gate, gate_rows, preferred_element_type=jnp.float32)
    grad_ffn_in = total + jnp.dot(grad_up, up_rows, preferred_element_type=jnp.float32)
    grad_gain_ffn_all = jnp.sum(normed_mid * grad_ffn_in, axis=0)
    grad_mid = grad_out.astype(jnp.float32) + norm_back(
        grad_ffn_in, normed_mid, rstd_mid, gain_ffn32
    )
    grad_branch = grad_mid.astype(jnp.bfloat16)
    grad_context = jnp.einsum(
        "td,ed->te", grad_branch, out_full, preferred_element_type=jnp.float32
    ).astype(jnp.bfloat16)
    grad_context_heads = lax.all_to_all(
        grad_context.reshape(cube), "seq", split_axis=2, concat_axis=1, tiled=True
    )

    def backward_one(item):
        query_seq, key_seq, value_seq, segment_ids, logsum_seq, grad_seq = item
        return attend_backward(
            query_seq.reshape(head_shape),
            key_seq.reshape(head_shape),
            value_seq.reshape(head_shape),
            segment_ids,
            logsum_seq,
            grad_seq.reshape(head_shape),
        )

    grad_query_heads, grad_key_heads, grad_value_heads = lax.map(
        backward_one, (query_heads, key_heads, value_heads, segments, logsum, grad_context_heads)
    )
    grad_query, grad_key, grad_value = (
        lax.all_to_all(grad_query_heads, "seq", split_axis=1, concat_axis=2, tiled=True),
        lax.all_to_all(grad_key_heads, "seq", split_axis=1, concat_axis=2, tiled=True),
        lax.all_to_all(grad_value_heads, "seq", split_axis=1, concat_axis=2, tiled=True),
    )
    grad_query = grad_query.reshape(count, width)
    grad_key = grad_key.reshape(count, width)
    grad_value = grad_value.reshape(count, width)
    query_rows, key_rows, value_rows = lax.all_gather(
        (w_query, w_key, w_value), ("dp", "seq"), axis=0, tiled=True
    )
    grad_in = jnp.einsum("te,de->td", grad_query, query_rows, preferred_element_type=jnp.float32)
    grad_memory_part = jnp.einsum(
        "te,de->td", grad_key, key_rows, preferred_element_type=jnp.float32
    )
    grad_memory_part = grad_memory_part + jnp.einsum(
        "te,de->td", grad_value, value_rows, preferred_element_type=jnp.float32
    )
    both_grads = jnp.stack((grad_in, grad_memory_part))
    grad_attn_in = both_grads[0]
    grad_memory = both_grads[1].reshape(cube)
    grad_gain_attn_all = jnp.sum(normed_in * grad_attn_in, axis=0)
    grad_hidden = (grad_mid + norm_back(grad_attn_in, normed_in, rstd_in, gain_attn_full)).reshape(
        cube
    )
    gain_attn_group, gain_ffn_group = lax.psum((grad_gain_attn_all, grad_gain_ffn_all), "seq")

    def regroup(values):
        return values.reshape(count, dp_count, groups, values.shape[1] // (dp_count * groups))

    left_parts = (
        lax.all_to_all(regroup(attn_in), "seq", split_axis=2, concat_axis=0, tiled=True),
        lax.all_to_all(regroup(memory_flat), "seq", split_axis=2, concat_axis=0, tiled=True),
        lax.all_to_all(regroup(context), "seq", split_axis=2, concat_axis=0, tiled=True),
        lax.all_to_all(regroup(grad_gate), "seq", split_axis=2, concat_axis=0, tiled=True),
        lax.all_to_all(regroup(grad_up), "seq", split_axis=2, concat_axis=0, tiled=True),
        lax.all_to_all(regroup(act), "seq", split_axis=2, concat_axis=0, tiled=True),
    )
    whole_count = count * groups
    attn_left, memory_left, context_left, gate_left, up_left, act_left = [
        part.reshape(whole_count, part.shape[1] * part.shape[3]) for part in left_parts
    ]
    query_right, key_right, value_right, branch_right, ffn_right, out_right = (
        lax.all_gather(grad_query, "seq", axis=0, tiled=True),
        lax.all_gather(grad_key, "seq", axis=0, tiled=True),
        lax.all_gather(grad_value, "seq", axis=0, tiled=True),
        lax.all_gather(grad_branch, "seq", axis=0, tiled=True),
        lax.all_gather(ffn_in, "seq", axis=0, tiled=True),
        lax.all_gather(grad_out, "seq", axis=0, tiled=True),
    )
    attn_block = 4 * share_d + 1
    ffn_block = 3 * share_f + 1
    whole_block = attn_block + ffn_block
    blocks = whole_block * lax.axis_size("dp") // whole_block
    all_grads = lax.psum_scatter(
        jnp.concatenate(
            [
                row_terms(attn_left, query_right, blocks, share_d),
                row_terms(memory_left, key_right, blocks, share_d),
                row_terms(memory_left, value_right, blocks, share_d),
                row_terms(context_left, branch_right, blocks, share_d),
                gain_terms(gain_attn_group, blocks),
            ]
            + [
                row_terms(gate_left, ffn_right, blocks, share_f),
                row_terms(up_left, ffn_right, blocks, share_f),
                row_terms(act_left, out_right, blocks, share_f),
                gain_terms(gain_ffn_group, blocks),
            ],
            axis=1,
        )
        .reshape(whole_block * lax.axis_size("dp"), width)
        .astype(jnp.bfloat16),
        "dp",
        scatter_dimension=0,
        tiled=True,
    ).astype(jnp.float32)
    attn_grads = all_grads[:attn_block]
    ffn_grads = all_grads[attn_block:]
    owner = lax.axis_index("dp") * groups + lax.axis_index("seq")
    grad_w_query = attn_grads[0:share_d]
    grad_w_key = attn_grads[share_d : 2 * share_d]
    grad_w_value = attn_grads[2 * share_d : 3 * share_d]
    grad_w_out = attn_grads[3 * share_d : 4 * share_d]
    grad_gain_attn = lax.dynamic_slice_in_dim(attn_grads[4 * share_d], owner * share_d, share_d)
    grad_w_gate = ffn_grads[0:share_f]
    grad_w_up = ffn_grads[share_f : 2 * share_f]
    grad_w_down = ffn_grads[2 * share_f : 3 * share_f]
    grad_gain_ffn = lax.dynamic_slice_in_dim(ffn_grads[3 * share_f], owner * share_d, share_d)
    return (
        layer_out,
        grad_hidden,
        grad_memory,
        grad_gain_attn,
        grad_w_query,
        grad_w_key,
        grad_w_value,
        grad_w_out,
        grad_gain_ffn,
        grad_w_gate,
        grad_w_up,
        grad_w_down,
    )


def solution(mesh):
    in_specs = (
        P("dp", "seq", None),
        P("dp", "seq", None),
        P("dp", None),
        P(("dp", "seq")),
        P(("dp", "seq"), None),
        P(("dp", "seq"), None),
        P(("dp", "seq"), None),
        P(("dp", "seq"), None),
        P(("dp", "seq")),
        P(("dp", "seq"), None),
        P(("dp", "seq"), None),
        P(("dp", "seq"), None),
        P("dp", "seq", None),
    )
    out_specs = (
        P("dp", "seq", None),
        P("dp", "seq", None),
        P("dp", "seq", None),
        P(("dp", "seq")),
        P(("dp", "seq"), None),
        P(("dp", "seq"), None),
        P(("dp", "seq"), None),
        P(("dp", "seq"), None),
        P(("dp", "seq")),
        P(("dp", "seq"), None),
        P(("dp", "seq"), None),
        P(("dp", "seq"), None),
    )
    return jax.shard_map(shards, mesh=mesh, in_specs=in_specs, out_specs=out_specs, check_vma=False)
```

profile of v0, /device:TPU:1, one launch (start us, length us, event | category | flops | bytes accessed | tf_op | source)
XLA Modules:
  0.0 3069.0 jit_solution(8761035630606516971)
XLA Ops:
  13.6 42.0 %all-reduce.5 = (bf16[2048]{0:T(1024)(128)(2,1)S(1)}, bf16[2048]{0:T(1024)(128)(2,1)}) all-reduce(bf16[2048]{0:T(1024)(128)(2,1)S(1)} %dynamic-update-slice, bf16[2048]{0:T(1024)(128)(2,1)S(1)} %dynamic-update-slice.1), channel_id=1, replica_groups=mesh['dp'=8,'seq'=4] {'dp','seq'}, use_global_device_ids=true, to_apply=%add | all-reduce | flops 4096 | bytes 16384
  56.8 34.4 %all-gather.18.cloned.1.call-done = bf16[2048,2048]{1,0:T(8,128)(2,1)} async-done(((bf16[64,2048]{1,0:T(8,128)(2,1)}), bf16[2048,2048]{1,0:T(8,128)(2,1)}) %all-gather.18.cloned.1.call-update) | async-done | bytes 8388624 | tf_op jit(solution)/shard_map/all_gather | solution.py:143
  132.5 63.4 %all-gather.20.cloned.1.call-done = bf16[2048,2048]{1,0:T(8,128)(2,1)} async-done(((bf16[64,2048]{1,0:T(8,128)(2,1)}), bf16[2048,2048]{1,0:T(8,128)(2,1)}) %all-gather.20.cloned.1.call-update) | async-done | bytes 8388624 | tf_op jit(solution)/shard_map/all_gather | solution.py:144
  244.7 63.4 %all-gather.22.cloned.1.call-done = bf16[2048,2048]{1,0:T(8,128)(2,1)} async-done(((bf16[64,2048]{1,0:T(8,128)(2,1)}), bf16[2048,2048]{1,0:T(8,128)(2,1)}) %all-gather.22.cloned.1.call-update) | async-done | bytes 8388624 | tf_op jit(solution)/shard_map/all_gather | solution.py:145
  384.7 41.9 %all-to-all-done.2 = bf16[4,2,131072]{2,1,0:T(2,128)(2,1)} async-done(((bf16[4,2,131072]{2,1,0:T(2,128)(2,1)}), bf16[4,2,131072]{2,1,0:T(2,128)(2,1)}, u32[]{:S(2)}, u32[]{:S(2)}) %all-to-all-start.2) | async-done | bytes 2097184 | tf_op jit(solution)/shard_map/all_to_all | solution.py:161
  448.9 74.5 %while.47 = (s32[]{:T(128)}, bf16[4,512,4,128]{3,2,1,0:T(4,128)(2,1)}, f32[4,4,512]{2,1,0:T(4,128)}, s32[4]{0:T(128)S(1)}, s32[2048]{0:T(1024)S(1)}, /*index=5*/...) while((s32[]{:T(128)}, ...), condition=%wide.region_4.5_spmd, body=%wide.region_1.4_spmd.sunk | while | flops 2201221632 | bytes 69291224 | solution.py:52
  560.0 67.4 %all-to-all-done.3 = bf16[4,2,131072]{2,1,0:T(2,128)(2,1)S(1)} async-done(((bf16[4,2,131072]{2,1,0:T(2,128)(2,1)}), bf16[4,2,131072]{2,1,0:T(2,128)(2,1)S(1)}, u32[]{:S(2)}, u32[]{:S(2)}) %all-to-all-start.3) | async-done | bytes 2097184 | tf_op jit(solution)/shard_map/all_to_all | solution.py:177
  663.2 23.0 reshape.356
  686.2 19.1 fusion.72
  705.3 70.9 %all-gather.40.cloned.1.call-done = bf16[32,172,2048]{2,1,0:T(8,128)(2,1)} async-done(((bf16[1,172,2048]{2,1,0:T(8,128)(2,1)}), bf16[32,172,2048]{2,1,0:T(8,128)(2,1)}) %all-gather.40.cloned.1.call-update) | async-done | bytes 22544400 | tf_op jit(solution)/shard_map/all_gather | solution.py:189
  776.2 22.2 reshape.358
  798.4 19.1 fusion.73
  817.5 104.3 %all-gather.42.cloned.1.call-done = bf16[32,172,2048]{2,1,0:T(8,128)(2,1)} async-done(((bf16[1,172,2048]{2,1,0:T(8,128)(2,1)}), bf16[32,172,2048]{2,1,0:T(8,128)(2,1)}) %all-gather.42.cloned.1.call-update) | async-done | bytes 22544400 | tf_op jit(solution)/shard_map/all_gather | solution.py:200
  921.8 22.4 reshape.360
  944.2 26.8 multiply_convert_fusion.1
  971.0 19.6 fusion.74
  990.7 21.8 multiply_reduce_fusion.1
  1061.5 87.5 %all-to-all-done.4 = bf16[4,2,131072]{2,1,0:T(2,128)(2,1)S(1)} async-done(((bf16[4,2,131072]{2,1,0:T(2,128)(2,1)}), bf16[4,2,131072]{2,1,0:T(2,128)(2,1)S(1)}, u32[]{:S(2)}, u32[]{:S(2)}) %all-to-all-start.4) | async-done | bytes 2097184 | tf_op jit(solution)/shard_map/all_to_all | solution.py:226
  1169.2 83.2 %all-to-all-done.9 = bf16[512,8,4,64]{0,3,1,2:T(8,128)(2,1)} async-done(((bf16[512,8,4,64]{0,3,1,2:T(8,128)(2,1)}), bf16[512,8,4,64]{0,3,1,2:T(8,128)(2,1)}, u32[]{:S(2)}, u32[]{:S(2)}) %all-to-all-start.9) | async-done | bytes 2097184 | tf_op jit(solution)/shard_map/all_to_all | solution.py:276
  1258.8 274.2 %while.48 = (s32[]{:T(128)}, f32[2048,4,128]{0,2,1:T(8,128)}, f32[2048,4,128]{0,2,1:T(8,128)}, bf16[4,512,4,128]{3,2,1,0:T(4,128)(2,1)}, s32[4]{0:T(128)S(1)}, /...) while((s32[]{:T(128)}, f32[2048,4,128]{0,2,1:T(8,128)}, ...), condition=%wide.region_9.10_spmd.clone, body=%wide.region_7.9_spmd.clone.sunk | while | flops 5440535040 | bytes 193538896 | solution.py:93
  1652.0 45.8 %all-to-all-done.5 = bf16[4,2,131072]{2,1,0:T(2,128)(2,1)} async-done(((bf16[4,2,131072]{2,1,0:T(2,128)(2,1)}), bf16[4,2,131072]{2,1,0:T(2,128)(2,1)}, u32[]{:S(2)}, u32[]{:S(2)}) %all-to-all-start.5) | async-done | bytes 2097184 | tf_op jit(solution)/shard_map/all_to_all | solution.py:245
  1701.8 29.0 reshape.365
  1745.4 54.4 %all-to-all-done.7 = bf16[4,2,131072]{2,1,0:T(2,128)(2,1)S(1)} async-done(((bf16[4,2,131072]{2,1,0:T(2,128)(2,1)}), bf16[4,2,131072]{2,1,0:T(2,128)(2,1)S(1)}, u32[]{:S(2)}, u32[]{:S(2)}) %all-to-all-start.7) | async-done | bytes 2097184 | tf_op jit(solution)/shard_map/all_to_all | solution.py:247
  1813.4 29.1 reshape.366
  1857.1 163.9 %all-to-all-done.11 = bf16[512,8,4,172]{0,1,3,2:T(8,128)(2,1)} async-done(((bf16[512,8,4,172]{0,1,3,2:T(8,128)(2,1)}), bf16[512,8,4,172]{0,1,3,2:T(8,128)(2,1)}, u32[]{:S(2)}, u32[]{:S(2)}) %all-to-all-start.11) | async-done | bytes 5636128 | tf_op jit(solution)/shard_map/all_to_all | solution.py:278
  2026.3 29.1 reshape.367
  2069.9 151.5 %all-to-all-done.12 = bf16[512,8,4,172]{0,1,3,2:T(8,128)(2,1)} async-done(((bf16[512,8,4,172]{0,1,3,2:T(8,128)(2,1)}), bf16[512,8,4,172]{0,1,3,2:T(8,128)(2,1)}, u32[]{:S(2)}, u32[]{:S(2)}) %all-to-all-start.12) | async-done | bytes 5636128 | tf_op jit(solution)/shard_map/all_to_all | solution.py:279
  2284.0 154.2 %all-reduce.4 = (bf16[2048]{0:T(1024)(128)(2,1)S(1)}, bf16[2048]{0:T(1024)(128)(2,1)S(1)}) all-reduce(f32[2048]{0:T(1024)S(1)} %get-tuple-element.284, f32[2048]{0:T(1024)S(1)} %copy-done.35), channel_id=1, replica_groups=mesh['dp'=8,'seq'=4] {'seq'}, use_global_device_ids=true, to_apply=%region_12.13 | all-reduce | flops 4096 | bytes 24576 | tf_op jit(solution)/shard_map/psum | solution.py:269
  2510.0 18.4 fusion.41
  2600.8 143.7 %concatenate.4 = bf16[8,774,2048]{2,1,0:T(8,128)(2,1)} concatenate(bf16[8,64,2048]{2,1,0:T(8,128)(2,1)} %fusion.51, bf16[8,64,2048]{2,1,0:T(8,128)(2,1)} %bitcast.343, bf16[8,64,2048]{2,1,0:T(8,128)(2,1)} %bitcast.344, bf16[8,64,2048]{2,1,0:T(8,128)(2,1)S(1)} %fusion.54, bf16[8,1,2048]{2,1,0:T(2,128)(2,1)S(1)} %broadcast_in_dim.83, bf16[8,172,2048]{2,1,0:T(8,128)(2,1)} %fusion.41, ...), dimensions={1} | concatenate | bytes 50724864 | tf_op jit(solution)/shard_map/concatenate | solution.py:299
  2744.5 25.0 convert_element_type.114
  2769.5 258.1 %fusion = bf16[784,2048]{1,0:T(8,128)(2,1)} fusion(bf16[6192,2048]{1,0:T(8,128)(2,1)} %convert_element_type.114), kind=kCustom, calls=%all-reduce-scatter | all-reduce-scatter fusion | flops 12845057 | bytes 28574208
  (375 shorter events, 1104.5 us)
Async XLA Ops:
  7.2 83.9 %all-gather.18.cloned.1.call-start = ((), (), s32[]{:S(2)}) async-start(), calls=%async_computation.14 | async-start | bytes 8650752 | tf_op jit(solution)/shard_map/all_gather | solution.py:143
  7.9 188.0 %all-gather.20.cloned.1.call-start = ((), (), s32[]{:S(2)}) async-start(), calls=%async_computation.15 | async-start | bytes 8650752 | tf_op jit(solution)/shard_map/all_gather | solution.py:144
  8.7 299.5 %all-gather.22.cloned.1.call-start = ((), (), s32[]{:S(2)}) async-start(), calls=%async_computation.16 | async-start | bytes 8650752 | tf_op jit(solution)/shard_map/all_gather | solution.py:145
  9.4 629.7 %all-gather.24.cloned.1.call-start = ((), (), s32[]{:S(2)}) async-start(), calls=%async_computation.17 | async-start | bytes 8650752 | tf_op jit(solution)/shard_map/all_gather | solution.py:181
  10.0 653.2 %all-gather.38.cloned.1.call-start = ((), (), s32[]{:S(2)}) async-start(), calls=%async_computation.24 | async-start | bytes 23789568 | tf_op jit(solution)/shard_map/all_gather | solution.py:189
  10.6 765.6 %all-gather.40.cloned.1.call-start = ((), (), s32[]{:S(2)}) async-start(), calls=%async_computation.25 | async-start | bytes 23789568 | tf_op jit(solution)/shard_map/all_gather | solution.py:189
  11.1 910.7 %all-gather.42.cloned.1.call-start = ((), (), s32[]{:S(2)}) async-start(), calls=%async_computation.26 | async-start | bytes 23789568 | tf_op jit(solution)/shard_map/all_gather | solution.py:200
  128.4 107.9 %all-to-all-start = ((bf16[4,2,131072]{2,1,0:T(2,128)(2,1)}), bf16[4,2,131072]{2,1,0:T(2,128)(2,1)S(1)}, u32[]{:S(2)}, u32[]{:S(2)}) async-start(bf16[4,2,131072]{2,1,0:T(2,128)(2,1)} %reshape.369), calls=%async_computation | async-start | bytes 4194304 | tf_op jit(solution)/shard_map/all_to_all | solution.py:155
  236.3 112.3 %all-to-all-start.1 = ((bf16[4,2,131072]{2,1,0:T(2,128)(2,1)}), bf16[4,2,131072]{2,1,0:T(2,128)(2,1)}, u32[]{:S(2)}, u32[]{:S(2)}) async-start(bf16[4,2,131072]{2,1,0:T(2,128)(2,1)} %reshape.371), calls=%async_computation.1 | async-start | bytes 4194304 | tf_op jit(solution)/shard_map/all_to_all | solution.py:158
  348.6 78.0 %all-to-all-start.2 = ((bf16[4,2,131072]{2,1,0:T(2,128)(2,1)}), bf16[4,2,131072]{2,1,0:T(2,128)(2,1)}, u32[]{:S(2)}, u32[]{:S(2)}) async-start(bf16[4,2,131072]{2,1,0:T(2,128)(2,1)} %reshape.373), calls=%async_computation.2 | async-start | bytes 4194304 | tf_op jit(solution)/shard_map/all_to_all | solution.py:161
  556.3 71.1 %all-to-all-start.3 = ((bf16[4,2,131072]{2,1,0:T(2,128)(2,1)}), bf16[4,2,131072]{2,1,0:T(2,128)(2,1)S(1)}, u32[]{:S(2)}, u32[]{:S(2)}) async-start(bf16[4,2,131072]{2,1,0:T(2,128)(2,1)} %reshape.375), calls=%async_computation.3 | async-start | bytes 4194304 | tf_op jit(solution)/shard_map/all_to_all | solution.py:177
  559.9 1950.0 %all-gather.34.cloned.1.call-start = ((), (), s32[]{:S(2)}) async-start(), calls=%async_computation.22 | async-start | bytes 10485760 | tf_op jit(solution)/shard_map/all_gather | solution.py:291
  658.0 392.9 %all-to-all-start.8 = ((bf16[512,8,4,64]{0,3,1,2:T(8,128)(2,1)}), bf16[512,8,4,64]{0,3,1,2:T(8,128)(2,1)}, u32[]{:S(2)}, u32[]{:S(2)}) async-start(bf16[512,8,4,64]{0,3,1,2:T(8,128)(2,1)} %copy.157), calls=%async_computation.8 | async-start | bytes 4194304 | tf_op jit(solution)/shard_map/all_to_all | solution.py:275
  662.4 1881.8 %all-gather.36.cloned.1.call-start = ((), (), s32[]{:S(2)}) async-start(), calls=%async_computation.23 | async-start | bytes 10485760 | tf_op jit(solution)/shard_map/all_gather | solution.py:292
  1050.8 98.1 %all-to-all-start.4 = ((bf16[4,2,131072]{2,1,0:T(2,128)(2,1)}), bf16[4,2,131072]{2,1,0:T(2,128)(2,1)S(1)}, u32[]{:S(2)}, u32[]{:S(2)}) async-start(bf16[4,2,131072]{2,1,0:T(2,128)(2,1)} %reshape.377), calls=%async_computation.4 | async-start | bytes 4194304 | tf_op jit(solution)/shard_map/all_to_all | solution.py:226
  1149.0 103.5 %all-to-all-start.9 = ((bf16[512,8,4,64]{0,3,1,2:T(8,128)(2,1)}), bf16[512,8,4,64]{0,3,1,2:T(8,128)(2,1)}, u32[]{:S(2)}, u32[]{:S(2)}) async-start(bf16[512,8,4,64]{0,3,1,2:T(8,128)(2,1)} %copy.160), calls=%async_computation.9 | async-start | bytes 4194304 | tf_op jit(solution)/shard_map/all_to_all | solution.py:276
  1153.5 1408.8 %all-gather.32.cloned.1.call-start = ((), (), s32[]{:S(2)}) async-start(), calls=%async_computation.21 | async-start | bytes 10485760 | tf_op jit(solution)/shard_map/all_gather | solution.py:290
  1252.4 307.5 %all-to-all-start.10 = ((bf16[512,8,4,64]{0,3,1,2:T(8,128)(2,1)}), bf16[512,8,4,64]{0,3,1,2:T(8,128)(2,1)}, u32[]{:S(2)}, u32[]{:S(2)}) async-start(bf16[512,8,4,64]{0,3,1,2:T(8,128)(2,1)} %copy.163), calls=%async_computation.10 | async-start | bytes 4194304 | tf_op jit(solution)/shard_map/all_to_all | solution.py:277
  1559.9 52.1 %all-to-all-start.6 = ((bf16[4,2,131072]{2,1,0:T(2,128)(2,1)}), bf16[4,2,131072]{2,1,0:T(2,128)(2,1)S(1)}, u32[]{:S(2)}, u32[]{:S(2)}) async-start(bf16[4,2,131072]{2,1,0:T(2,128)(2,1)} %reshape.381), calls=%async_computation.6 | async-start | bytes 4194304 | tf_op jit(solution)/shard_map/all_to_all | solution.py:246
  1612.0 85.7 %all-to-all-start.5 = ((bf16[4,2,131072]{2,1,0:T(2,128)(2,1)}), bf16[4,2,131072]{2,1,0:T(2,128)(2,1)}, u32[]{:S(2)}, u32[]{:S(2)}) async-start(bf16[4,2,131072]{2,1,0:T(2,128)(2,1)} %reshape.379), calls=%async_computation.5 | async-start | bytes 4194304 | tf_op jit(solution)/shard_map/all_to_all | solution.py:245
  1616.5 954.4 %all-gather.28.cloned.1.call-start = ((), (), s32[]{:S(2)}) async-start(), calls=%async_computation.19 | async-start | bytes 10485760 | tf_op jit(solution)/shard_map/all_gather | solution.py:288
  1697.8 102.0 %all-to-all-start.7 = ((bf16[4,2,131072]{2,1,0:T(2,128)(2,1)}), bf16[4,2,131072]{2,1,0:T(2,128)(2,1)S(1)}, u32[]{:S(2)}, u32[]{:S(2)}) async-start(bf16[4,2,131072]{2,1,0:T(2,128)(2,1)} %reshape.383), calls=%async_computation.7 | async-start | bytes 4194304 | tf_op jit(solution)/shard_map/all_to_all | solution.py:247
  1799.8 221.2 %all-to-all-start.11 = ((bf16[512,8,4,172]{0,1,3,2:T(8,128)(2,1)}), bf16[512,8,4,172]{0,1,3,2:T(8,128)(2,1)}, u32[]{:S(2)}, u32[]{:S(2)}) async-start(bf16[512,8,4,172]{0,1,3,2:T(8,128)(2,1)} %copy.166), calls=%async_computation.11 | async-start | bytes 11272192 | tf_op jit(solution)/shard_map/all_to_all | solution.py:278
  1804.9 775.9 %all-gather.30.cloned.1.call-start = ((), (), s32[]{:S(2)}) async-start(), calls=%async_computation.20 | async-start | bytes 10485760 | tf_op jit(solution)/shard_map/all_gather | solution.py:289
  2020.9 200.5 %all-to-all-start.12 = ((bf16[512,8,4,172]{0,1,3,2:T(8,128)(2,1)}), bf16[512,8,4,172]{0,1,3,2:T(8,128)(2,1)}, u32[]{:S(2)}, u32[]{:S(2)}) async-start(bf16[512,8,4,172]{0,1,3,2:T(8,128)(2,1)} %copy.169), calls=%async_computation.12 | async-start | bytes 11272192 | tf_op jit(solution)/shard_map/all_to_all | solution.py:279
  2221.4 270.8 %all-to-all-start.13 = ((bf16[512,8,4,172]{0,1,3,2:T(8,128)(2,1)}), bf16[512,8,4,172]{0,1,3,2:T(8,128)(2,1)}, u32[]{:S(2)}, u32[]{:S(2)}) async-start(bf16[512,8,4,172]{0,1,3,2:T(8,128)(2,1)} %copy.172), calls=%async_computation.13 | async-start | bytes 11272192 | tf_op jit(solution)/shard_map/all_to_all | solution.py:280
  2226.5 364.0 %all-gather.26.cloned.1.call-start = ((), (), s32[]{:S(2)}) async-start(), calls=%async_computation.18 | async-start | bytes 10485760 | tf_op jit(solution)/shard_map/all_gather | solution.py:287
  2769.5 263.6 %copy-start.25 = (f32[2048]{0:T(1024)S(1)}, f32[2048]{0:T(1024)}, u32[]{:S(2)}) copy-start(f32[2048]{0:T(1024)} %copy-done.23) | copy-start | bytes 24580
  2769.5 263.6 %copy-start.29 = (f32[512]{0:T(512)S(1)}, f32[512]{0:T(512)}, u32[]{:S(2)}) copy-start(f32[512]{0:T(512)} %copy-done.26) | copy-start | bytes 6148
  2769.5 263.6 %copy-start.31 = (f32[512]{0:T(512)S(1)}, f32[512]{0:T(512)}, u32[]{:S(2)}) copy-start(f32[512]{0:T(512)} %copy-done.30) | copy-start | bytes 6148
  2769.5 263.6 %copy-start.34 = (f32[512]{0:T(512)S(1)}, f32[512]{0:T(512)}, u32[]{:S(2)}) copy-start(f32[512]{0:T(512)} %broadcast_multiply_fusion) | copy-start | bytes 6148
  3028.7 12.3 collective-permute-start
  (46 other events, 1755.5 us)
Sparse Core Ops, SparseCore 0:
  11.0 80.1 all-gather.17
  94.0 101.7 all-gather.19
  198.8 109.2 all-gather.21
  310.9 108.5 all-gather.23
  422.2 161.5 all-gather.37
  586.4 189.6 all-gather.39
  779.0 142.7 all-gather.41
  923.4 165.5 all-gather.33
  1090.5 250.3 all-gather.35
  1342.3 147.7 all-gather.31
  1625.1 307.7 all-gather.27
  1934.3 272.3 all-gather.29
  2273.2 213.7 all-gather.25
where the time goes:
time: 3090 us; the launch traced here: 3070 us
  waiting for transfers between devices  1050 us (34%)
  local copies, waits for them, and re-layouts  719 us (23%)
  matrix products  509 us (16%)
  blocking collectives  454 us (15%)
  other arithmetic  230 us (7%)
  starting transfers between devices  73.9 us (2%)
    unnamed x2, blocking collectives  300 us
    unnamed x119, local copies, waits for them, and re-layouts  203 us
    all_to_all x1, waiting for transfers between devices, shards(): lax.all_to_all(regroup(grad_gate), 'seq', split_axis=2, concat_axis=0, ti...  164 us
    psum x1, blocking collectives, shards(): lax.psum((grad_gain_attn_all, grad_gain_ffn_all), 'seq')  154 us
    all_to_all x1, waiting for transfers between devices, shards(): lax.all_to_all(regroup(grad_up), 'seq', split_axis=2, concat_axis=0, tile...  152 us
    concatenate x1, local copies, waits for them, and re-layouts, shards(): jnp.concatenate([row_terms(attn_left, query_right, blocks, share_d), row_...  144 us
    reshape x6, local copies, waits for them, and re-layouts, regroup(): values.reshape(count, dp_count, groups, values.shape[1] // (dp_count * gr...  131 us
    unnamed x11, other arithmetic  118 us
  transfers between devices with their start and end apart: 28, of which 14 were waited for; matrix products, arithmetic and copies ran while one was open for 41% of the time, Pallas kernels for 0%

commit v1 on v0

--- a/solution.py
+++ b/solution.py
@@ -1,3 +1,4 @@
+import functools
 import jax
 import jax.numpy as jnp
 from jax import lax
@@ -6,6 +7,35 @@
 HEAD_DIM = 128
 EPSILON = 1e-06
 MASKED = -1e30
+
+
+def try_all_values_here(state, where_dim, field_in):
+    front, plain = (state.shape[:where_dim], state.shape[where_dim + 1 :])
+    return jnp.moveaxis(state.reshape(*front, field_in, -1, *plain), where_dim, 0)
+
+
+def reach_the_vectors(inp, pos_dim):
+    s_next = list(inp.shape[1:])
+    s_next[pos_dim] *= inp.shape[0]
+    return jnp.moveaxis(inp, 0, pos_dim).reshape(s_next)
+
+
+def _detail_sections(xin, mesh_dim, target, array_in):
+    passed, block_out = (lax.axis_size(mesh_dim), lax.axis_index(mesh_dim))
+    block_next = try_all_values_here(xin, target, passed)
+    series = [block_next[block_out]]
+    for no in range(1, passed):
+        y_new = block_next[block_out ^ no]
+        series.append(
+            lax.ppermute(
+                y_new, axis_name=mesh_dim, perm=[(tick, tick ^ no) for tick in range(passed)]
+            )
+        )
+    block_next = jnp.stack(series)[block_out ^ jnp.arange(passed)]
+    return reach_the_vectors(block_next, array_in)
+
+
+copies_measure = functools.partial(_detail_sections, mesh_dim="seq", target=2, array_in=0)
 
 
 def rms_scale(values):
@@ -275,7 +305,7 @@
         lax.all_to_all(regroup(attn_in), "seq", split_axis=2, concat_axis=0, tiled=True),
         lax.all_to_all(regroup(memory_flat), "seq", split_axis=2, concat_axis=0, tiled=True),
         lax.all_to_all(regroup(context), "seq", split_axis=2, concat_axis=0, tiled=True),
-        lax.all_to_all(regroup(grad_gate), "seq", split_axis=2, concat_axis=0, tiled=True),
+        copies_measure(regroup(grad_gate)),
         lax.all_to_all(regroup(grad_up), "seq", split_axis=2, concat_axis=0, tiled=True),
         lax.all_to_all(regroup(act), "seq", split_axis=2, concat_axis=0, tiled=True),
     )

time: 3090 us -> 2960 us (0.958)
  blocking collectives: 454 us -> 369 us
  waiting for transfers between devices: 1050 us -> 1010 us
    all_to_all x1 -> x0, waiting for transfers between devices: 164 us -> none  [shards(): lax.all_to_all(regroup(grad_gate), 'seq', split_axis=2, concat_axis=0, ti...]
    ppermute x0 -> x3, waiting for transfers between devices: none -> 91.9 us  [_detail_sections(): lax.ppermute(y_new, axis_name=mesh_dim, perm=[(tick, tick ^ no) for tick...]
    psum x1, blocking collectives: 154 us -> 73.7 us  [shards(): lax.psum((grad_gain_attn_all, grad_gain_ffn_all), 'seq')]
    all_to_all x1, waiting for transfers between devices: 0.01 us -> 74.9 us  [shards(): lax.all_to_all(regroup(context), 'seq', split_axis=2, concat_axis=0, tile...]
    all_to_all x1, waiting for transfers between devices: 54.4 us -> 3.39 us  [shards(): lax.all_to_all(grad_value_heads, 'seq', split_axis=1, concat_axis=2, tile...]
    reshape x6 -> x4, local copies, waits for them, and re-layouts: 131 us -> 87.1 us  [regroup(): values.reshape(count, dp_count, groups, values.shape[1] // (dp_count * gr...]
    unnamed x119 -> x107, local copies, waits for them, and re-layouts: 203 us -> 205 us
    unnamed x11 -> x10, other arithmetic: 118 us -> 118 us
  transfers between devices with their start and end apart: 28 -> 30, of which waited for: 14 -> 16; matrix products, arithmetic and copies ran while one was open for 41% -> 43% of each run, Pallas kernels for 0% -> 0%
where the time goes in v1:
time: 2960 us; the launch traced here: 2940 us
  waiting for transfers between devices  1010 us (34%)
  local copies, waits for them, and re-layouts  707 us (24%)
  matrix products  518 us (18%)
  blocking collectives  369 us (12%)
  other arithmetic  236 us (8%)
  starting transfers between devices  72.8 us (2%)
    unnamed x2, blocking collectives  296 us
    unnamed x107, local copies, waits for them, and re-layouts  205 us
    all_to_all x1, waiting for transfers between devices, shards(): lax.all_to_all(regroup(grad_up), 'seq', split_axis=2, concat_axis=0, tile...  168 us
    concatenate x1, local copies, waits for them, and re-layouts, shards(): jnp.concatenate([row_terms(attn_left, query_right, blocks, share_d), row_...  148 us
    unnamed x10, other arithmetic  118 us
    all_gather x1, waiting for transfers between devices, shards(): lax.all_gather(w_down, ('dp', 'seq'), axis=0, tiled=True)  104 us
    dot_general x7, matrix products, row_terms(): jnp.einsum('tk,td->kd', left, right, preferred_element_type=jnp.float32)  93.9 us
    ppermute x3, waiting for transfers between devices, _detail_sections(): lax.ppermute(y_new, axis_name=mesh_dim, perm=[(tick, tick ^ no) for tick...  91.9 us
  transfers between devices with their start and end apart: 30, of which 16 were waited for; matrix products, arithmetic and copies ran while one was open for 43% of the time, Pallas kernels for 0%

profile of v1, /device:TPU:1, one launch (start us, length us, event | category | flops | bytes accessed | tf_op | source)
XLA Modules:
  0.0 2943.0 jit_solution(6151377399203111694)
XLA Ops:
  13.6 42.0 %all-reduce.5 = (bf16[2048]{0:T(1024)(128)(2,1)S(1)}, bf16[2048]{0:T(1024)(128)(2,1)}) all-reduce(bf16[2048]{0:T(1024)(128)(2,1)S(1)} %dynamic-update-slice, bf16[2048]{0:T(1024)(128)(2,1)S(1)} %dynamic-update-slice.1), channel_id=1, replica_groups=mesh['dp'=8,'seq'=4] {'dp','seq'}, use_global_device_ids=true, to_apply=%add | all-reduce | flops 4096 | bytes 16384
  56.8 34.4 %all-gather.18.cloned.1.call-done = bf16[2048,2048]{1,0:T(8,128)(2,1)} async-done(((bf16[64,2048]{1,0:T(8,128)(2,1)}), bf16[2048,2048]{1,0:T(8,128)(2,1)}) %all-gather.18.cloned.1.call-update) | async-done | bytes 8388624 | tf_op jit(solution)/shard_map/all_gather | solution.py:173
  132.2 63.3 %all-gather.20.cloned.1.call-done = bf16[2048,2048]{1,0:T(8,128)(2,1)} async-done(((bf16[64,2048]{1,0:T(8,128)(2,1)}), bf16[2048,2048]{1,0:T(8,128)(2,1)}) %all-gather.20.cloned.1.call-update) | async-done | bytes 8388624 | tf_op jit(solution)/shard_map/all_gather | solution.py:174
  245.0 63.4 %all-gather.22.cloned.1.call-done = bf16[2048,2048]{1,0:T(8,128)(2,1)} async-done(((bf16[64,2048]{1,0:T(8,128)(2,1)}), bf16[2048,2048]{1,0:T(8,128)(2,1)}) %all-gather.22.cloned.1.call-update) | async-done | bytes 8388624 | tf_op jit(solution)/shard_map/all_gather | solution.py:175
  385.0 41.9 %all-to-all-done.2 = bf16[4,2,131072]{2,1,0:T(2,128)(2,1)} async-done(((bf16[4,2,131072]{2,1,0:T(2,128)(2,1)}), bf16[4,2,131072]{2,1,0:T(2,128)(2,1)}, u32[]{:S(2)}, u32[]{:S(2)}) %all-to-all-start.2) | async-done | bytes 2097184 | tf_op jit(solution)/shard_map/all_to_all | solution.py:191
  449.3 74.4 %while.47 = (s32[]{:T(128)}, bf16[4,512,4,128]{3,2,1,0:T(4,128)(2,1)}, f32[4,4,512]{2,1,0:T(4,128)}, s32[4]{0:T(128)S(1)}, s32[2048]{0:T(1024)S(1)}, /*index=5*/...) while((s32[]{:T(128)}, ...), condition=%wide.region_4.5_spmd, body=%wide.region_1.4_spmd.sunk | while | flops 2201221632 | bytes 69291224 | solution.py:82
  560.5 67.3 %all-to-all-done.3 = bf16[4,2,131072]{2,1,0:T(2,128)(2,1)S(1)} async-done(((bf16[4,2,131072]{2,1,0:T(2,128)(2,1)}), bf16[4,2,131072]{2,1,0:T(2,128)(2,1)S(1)}, u32[]{:S(2)}, u32[]{:S(2)}) %all-to-all-start.3) | async-done | bytes 2097184 | tf_op jit(solution)/shard_map/all_to_all | solution.py:207
  651.8 23.1 reshape.381
  674.9 19.3 fusion.75
  694.2 46.0 %all-gather.40.cloned.1.call-done = bf16[32,172,2048]{2,1,0:T(8,128)(2,1)} async-done(((bf16[1,172,2048]{2,1,0:T(8,128)(2,1)}), bf16[32,172,2048]{2,1,0:T(8,128)(2,1)}) %all-gather.40.cloned.1.call-update) | async-done | bytes 22544400 | tf_op jit(solution)/shard_map/all_gather | solution.py:219
  740.1 22.2 reshape.383
  762.4 19.0 fusion.76
  781.4 104.4 %all-gather.42.cloned.1.call-done = bf16[32,172,2048]{2,1,0:T(8,128)(2,1)} async-done(((bf16[1,172,2048]{2,1,0:T(8,128)(2,1)}), bf16[32,172,2048]{2,1,0:T(8,128)(2,1)}) %all-gather.42.cloned.1.call-update) | async-done | bytes 22544400 | tf_op jit(solution)/shard_map/all_gather | solution.py:230
  885.8 22.4 reshape.385
  908.2 26.8 multiply_convert_fusion.1
  935.1 19.6 fusion.77
  954.7 21.9 multiply_reduce_fusion.1
  1030.2 83.2 %all-to-all-done.4 = bf16[4,2,131072]{2,1,0:T(2,128)(2,1)} async-done(((bf16[4,2,131072]{2,1,0:T(2,128)(2,1)}), bf16[4,2,131072]{2,1,0:T(2,128)(2,1)}, u32[]{:S(2)}, u32[]{:S(2)}) %all-to-all-start.4) | async-done | bytes 2097184 | tf_op jit(solution)/shard_map/all_to_all | solution.py:256
  1134.0 273.0 %while.48 = (s32[]{:T(128)}, f32[2048,4,128]{0,2,1:T(8,128)}, f32[2048,4,128]{0,2,1:T(8,128)}, bf16[4,512,4,128]{3,2,1,0:T(4,128)(2,1)}, s32[4]{0:T(128)S(1)}, /...) while((s32[]{:T(128)}, f32[2048,4,128]{0,2,1:T(8,128)}, ...), condition=%wide.region_9.10_spmd.clone, body=%wide.region_7.9_spmd.clone.sunk | while | flops 5440535040 | bytes 193538896 | solution.py:123
  1445.1 40.7 %all-to-all-done.6 = bf16[4,2,131072]{2,1,0:T(2,128)(2,1)S(1)} async-done(((bf16[4,2,131072]{2,1,0:T(2,128)(2,1)}), bf16[4,2,131072]{2,1,0:T(2,128)(2,1)S(1)}, u32[]{:S(2)}, u32[]{:S(2)}) %all-to-all-start.6) | async-done | bytes 2097184 | tf_op jit(solution)/shard_map/all_to_all | solution.py:276
  1502.1 69.5 %all-to-all-done.9 = bf16[512,8,4,64]{0,3,1,2:T(8,128)(2,1)} async-done(((bf16[512,8,4,64]{0,3,1,2:T(8,128)(2,1)}), bf16[512,8,4,64]{0,3,1,2:T(8,128)(2,1)}, u32[]{:S(2)}, u32[]{:S(2)}) %all-to-all-start.9) | async-done | bytes 2097184 | tf_op jit(solution)/shard_map/all_to_all | solution.py:306
  1599.0 74.9 %all-to-all-done.10 = bf16[512,8,4,64]{0,3,1,2:T(8,128)(2,1)} async-done(((bf16[512,8,4,64]{0,3,1,2:T(8,128)(2,1)}), bf16[512,8,4,64]{0,3,1,2:T(8,128)(2,1)}, u32[]{:S(2)}, u32[]{:S(2)}) %all-to-all-start.10) | async-done | bytes 2097184 | tf_op jit(solution)/shard_map/all_to_all | solution.py:307
  1705.2 50.2 %all-to-all-done.5 = bf16[4,2,131072]{2,1,0:T(2,128)(2,1)} async-done(((bf16[4,2,131072]{2,1,0:T(2,128)(2,1)}), bf16[4,2,131072]{2,1,0:T(2,128)(2,1)}, u32[]{:S(2)}, u32[]{:S(2)}) %all-to-all-start.5) | async-done | bytes 2097184 | tf_op jit(solution)/shard_map/all_to_all | solution.py:275
  1759.2 29.0 reshape.390
  1864.5 29.1 reshape.391
  1908.1 168.1 %all-to-all-done.11 = bf16[512,8,4,172]{0,1,3,2:T(8,128)(2,1)} async-done(((bf16[512,8,4,172]{0,1,3,2:T(8,128)(2,1)}), bf16[512,8,4,172]{0,1,3,2:T(8,128)(2,1)}, u32[]{:S(2)}, u32[]{:S(2)}) %all-to-all-start.11) | async-done | bytes 5636128 | tf_op jit(solution)/shard_map/all_to_all | solution.py:309
  2081.4 19.8 fusion.57
  2102.0 91.9 %collective-permute-done.1 = bf16[512,8,1,172]{0,1,3,2:T(8,128)(2,1)} collective-permute-done((bf16[512,8,1,172]{0,1,3,2:T(8,128)(2,1)}, bf16[512,8,1,172]{0,1,3,2:T(8,128)(2,1)}, u32[]{:S(2)}, u32[]{:S(2)}) %collective-permute-start.1) | collective-permute-done | bytes 1409056 | tf_op jit(solution)/shard_map/ppermute | solution.py:30
  2273.8 73.7 %all-reduce.4 = (bf16[2048]{0:T(1024)(128)(2,1)S(1)}, bf16[2048]{0:T(1024)(128)(2,1)S(1)}) all-reduce(f32[2048]{0:T(1024)S(1)} %get-tuple-element.284, f32[2048]{0:T(1024)S(1)} %copy-done.32), channel_id=1, replica_groups=mesh['dp'=8,'seq'=4] {'seq'}, use_global_device_ids=true, to_apply=%region_12.13 | all-reduce | flops 4096 | bytes 24576 | tf_op jit(solution)/shard_map/psum | solution.py:299
  2475.1 147.6 %concatenate.4 = bf16[8,774,2048]{2,1,0:T(8,128)(2,1)} concatenate(bf16[8,64,2048]{2,1,0:T(8,128)(2,1)} %fusion.51, bf16[8,64,2048]{2,1,0:T(8,128)(2,1)} %bitcast.358, bf16[8,64,2048]{2,1,0:T(8,128)(2,1)} %bitcast.359, bf16[8,64,2048]{2,1,0:T(8,128)(2,1)} %fusion.54, bf16[8,1,2048]{2,1,0:T(2,128)(2,1)S(1)} %broadcast_in_dim.84, bf16[8,172,2048]{2,1,0:T(8,128)(2,1)} %fusion.41, ...), dimensions={1} | concatenate | bytes 50724864 | tf_op jit(solution)/shard_map/concatenate | solution.py:329
  2622.7 25.0 convert_element_type.114
  2647.7 253.6 %fusion = bf16[784,2048]{1,0:T(8,128)(2,1)} fusion(bf16[6192,2048]{1,0:T(8,128)(2,1)} %convert_element_type.114), kind=kCustom, calls=%all-reduce-scatter | all-reduce-scatter fusion | flops 12845057 | bytes 28574208
  (375 shorter events, 1120.1 us)
Async XLA Ops:
  7.2 83.9 %all-gather.18.cloned.1.call-start = ((), (), s32[]{:S(2)}) async-start(), calls=%async_computation.13 | async-start | bytes 8650752 | tf_op jit(solution)/shard_map/all_gather | solution.py:173
  7.9 187.6 %all-gather.20.cloned.1.call-start = ((), (), s32[]{:S(2)}) async-start(), calls=%async_computation.14 | async-start | bytes 8650752 | tf_op jit(solution)/shard_map/all_gather | solution.py:174
  8.7 299.7 %all-gather.22.cloned.1.call-start = ((), (), s32[]{:S(2)}) async-start(), calls=%async_computation.15 | async-start | bytes 8650752 | tf_op jit(solution)/shard_map/all_gather | solution.py:175
  9.4 630.0 %all-gather.24.cloned.1.call-start = ((), (), s32[]{:S(2)}) async-start(), calls=%async_computation.16 | async-start | bytes 8650752 | tf_op jit(solution)/shard_map/all_gather | solution.py:211
  10.0 641.8 %all-gather.38.cloned.1.call-start = ((), (), s32[]{:S(2)}) async-start(), calls=%async_computation.23 | async-start | bytes 23789568 | tf_op jit(solution)/shard_map/all_gather | solution.py:219
  10.6 729.6 %all-gather.40.cloned.1.call-start = ((), (), s32[]{:S(2)}) async-start(), calls=%async_computation.24 | async-start | bytes 23789568 | tf_op jit(solution)/shard_map/all_gather | solution.py:219
  11.1 874.6 %all-gather.42.cloned.1.call-start = ((), (), s32[]{:S(2)}) async-start(), calls=%async_computation.25 | async-start | bytes 23789568 | tf_op jit(solution)/shard_map/all_gather | solution.py:230
  128.4 107.6 %all-to-all-start = ((bf16[4,2,131072]{2,1,0:T(2,128)(2,1)}), bf16[4,2,131072]{2,1,0:T(2,128)(2,1)S(1)}, u32[]{:S(2)}, u32[]{:S(2)}) async-start(bf16[4,2,131072]{2,1,0:T(2,128)(2,1)} %reshape.393), calls=%async_computation | async-start | bytes 4194304 | tf_op jit(solution)/shard_map/all_to_all | solution.py:185
  236.1 112.8 %all-to-all-start.1 = ((bf16[4,2,131072]{2,1,0:T(2,128)(2,1)}), bf16[4,2,131072]{2,1,0:T(2,128)(2,1)}, u32[]{:S(2)}, u32[]{:S(2)}) async-start(bf16[4,2,131072]{2,1,0:T(2,128)(2,1)} %reshape.395), calls=%async_computation.1 | async-start | bytes 4194304 | tf_op jit(solution)/shard_map/all_to_all | solution.py:188
  348.9 78.0 %all-to-all-start.2 = ((bf16[4,2,131072]{2,1,0:T(2,128)(2,1)}), bf16[4,2,131072]{2,1,0:T(2,128)(2,1)}, u32[]{:S(2)}, u32[]{:S(2)}) async-start(bf16[4,2,131072]{2,1,0:T(2,128)(2,1)} %reshape.397), calls=%async_computation.2 | async-start | bytes 4194304 | tf_op jit(solution)/shard_map/all_to_all | solution.py:191
  556.8 71.0 %all-to-all-start.3 = ((bf16[4,2,131072]{2,1,0:T(2,128)(2,1)}), bf16[4,2,131072]{2,1,0:T(2,128)(2,1)S(1)}, u32[]{:S(2)}, u32[]{:S(2)}) async-start(bf16[4,2,131072]{2,1,0:T(2,128)(2,1)} %reshape.399), calls=%async_computation.3 | async-start | bytes 4194304 | tf_op jit(solution)/shard_map/all_to_all | solution.py:207
  560.4 1663.1 %all-gather.34.cloned.1.call-start = ((), (), s32[]{:S(2)}) async-start(), calls=%async_computation.21 | async-start | bytes 10485760 | tf_op jit(solution)/shard_map/all_gather | solution.py:321
  651.0 1762.4 %all-gather.36.cloned.1.call-start = ((), (), s32[]{:S(2)}) async-start(), calls=%async_computation.22 | async-start | bytes 10485760 | tf_op jit(solution)/shard_map/all_gather | solution.py:322
  1018.4 95.0 %all-to-all-start.4 = ((bf16[4,2,131072]{2,1,0:T(2,128)(2,1)}), bf16[4,2,131072]{2,1,0:T(2,128)(2,1)}, u32[]{:S(2)}, u32[]{:S(2)}) async-start(bf16[4,2,131072]{2,1,0:T(2,128)(2,1)} %reshape.401), calls=%async_computation.4 | async-start | bytes 4194304 | tf_op jit(solution)/shard_map/all_to_all | solution.py:256
  1022.8 1408.7 %all-gather.32.cloned.1.call-start = ((), (), s32[]{:S(2)}) async-start(), calls=%async_computation.20 | async-start | bytes 10485760 | tf_op jit(solution)/shard_map/all_gather | solution.py:320
  1113.4 320.6 %all-to-all-start.8 = ((bf16[512,8,4,64]{0,3,1,2:T(8,128)(2,1)}), bf16[512,8,4,64]{0,3,1,2:T(8,128)(2,1)}, u32[]{:S(2)}, u32[]{:S(2)}) async-start(bf16[512,8,4,64]{0,3,1,2:T(8,128)(2,1)} %copy.170), calls=%async_computation.8 | async-start | bytes 4194304 | tf_op jit(solution)/shard_map/all_to_all | solution.py:305
  1433.9 51.8 %all-to-all-start.6 = ((bf16[4,2,131072]{2,1,0:T(2,128)(2,1)}), bf16[4,2,131072]{2,1,0:T(2,128)(2,1)S(1)}, u32[]{:S(2)}, u32[]{:S(2)}) async-start(bf16[4,2,131072]{2,1,0:T(2,128)(2,1)} %reshape.405), calls=%async_computation.6 | async-start | bytes 4194304 | tf_op jit(solution)/shard_map/all_to_all | solution.py:276
  1485.7 85.8 %all-to-all-start.9 = ((bf16[512,8,4,64]{0,3,1,2:T(8,128)(2,1)}), bf16[512,8,4,64]{0,3,1,2:T(8,128)(2,1)}, u32[]{:S(2)}, u32[]{:S(2)}) async-start(bf16[512,8,4,64]{0,3,1,2:T(8,128)(2,1)} %copy.173), calls=%async_computation.9 | async-start | bytes 4194304 | tf_op jit(solution)/shard_map/all_to_all | solution.py:306
  1490.2 951.4 %all-gather.28.cloned.1.call-start = ((), (), s32[]{:S(2)}) async-start(), calls=%async_computation.18 | async-start | bytes 10485760 | tf_op jit(solution)/shard_map/all_gather | solution.py:318
  1571.6 102.3 %all-to-all-start.10 = ((bf16[512,8,4,64]{0,3,1,2:T(8,128)(2,1)}), bf16[512,8,4,64]{0,3,1,2:T(8,128)(2,1)}, u32[]{:S(2)}, u32[]{:S(2)}) async-start(bf16[512,8,4,64]{0,3,1,2:T(8,128)(2,1)} %copy.176), calls=%async_computation.10 | async-start | bytes 4194304 | tf_op jit(solution)/shard_map/all_to_all | solution.py:307
  1673.9 81.5 %all-to-all-start.5 = ((bf16[4,2,131072]{2,1,0:T(2,128)(2,1)}), bf16[4,2,131072]{2,1,0:T(2,128)(2,1)}, u32[]{:S(2)}, u32[]{:S(2)}) async-start(bf16[4,2,131072]{2,1,0:T(2,128)(2,1)} %reshape.403), calls=%async_computation.5 | async-start | bytes 4194304 | tf_op jit(solution)/shard_map/all_to_all | solution.py:275
  1755.4 50.7 %all-to-all-start.7 = ((bf16[4,2,131072]{2,1,0:T(2,128)(2,1)}), bf16[4,2,131072]{2,1,0:T(2,128)(2,1)S(1)}, u32[]{:S(2)}, u32[]{:S(2)}) async-start(bf16[4,2,131072]{2,1,0:T(2,128)(2,1)} %reshape.407), calls=%async_computation.7 | async-start | bytes 4194304 | tf_op jit(solution)/shard_map/all_to_all | solution.py:277
  1806.1 270.1 %all-to-all-start.11 = ((bf16[512,8,4,172]{0,1,3,2:T(8,128)(2,1)}), bf16[512,8,4,172]{0,1,3,2:T(8,128)(2,1)}, u32[]{:S(2)}, u32[]{:S(2)}) async-start(bf16[512,8,4,172]{0,1,3,2:T(8,128)(2,1)} %copy.186), calls=%async_computation.11 | async-start | bytes 11272192 | tf_op jit(solution)/shard_map/all_to_all | solution.py:309
  1811.3 640.1 %all-gather.30.cloned.1.call-start = ((), (), s32[]{:S(2)}) async-start(), calls=%async_computation.19 | async-start | bytes 10485760 | tf_op jit(solution)/shard_map/all_gather | solution.py:319
  1857.2 244.8 %collective-permute-start = (bf16[512,8,1,172]{0,1,3,2:T(8,128)(2,1)S(1)}, bf16[512,8,1,172]{0,1,3,2:T(8,128)(2,1)}, u32[]{:S(2)}, u32[]{:S(2)}) collective-permute-start(bf16[512,8,1,172]{0,1,3,2:T(8,128)(2,1)S(1)} %bitcast.364), channel_id=1, source_target_pairs={{0,1},{1,0},{2,3},{3,2},{4,5},{5,4},{6,7},{7,6},{8,9},{9,8},{10,11... | collective-permute-start | bytes 4227080 | tf_op jit(solution)/shard_map/ppermute | solution.py:30
  1860.4 333.5 %collective-permute-start.1 = (bf16[512,8,1,172]{0,1,3,2:T(8,128)(2,1)}, bf16[512,8,1,172]{0,1,3,2:T(8,128)(2,1)}, u32[]{:S(2)}, u32[]{:S(2)}) collective-permute-start(bf16[512,8,1,172]{0,1,3,2:T(8,128)(2,1)} %bitcast.280), channel_id=1, source_target_pairs={{0,2},{1,3},{2,0},{3,1},{4,6},{5,7},{6,4},{7,5},{8,10},{9,11},{10,... | collective-permute-start | bytes 4227080 | tf_op jit(solution)/shard_map/ppermute | solution.py:30
  1864.3 329.6 %collective-permute-start.2 = (bf16[512,8,1,172]{0,1,3,2:T(8,128)(2,1)}, bf16[512,8,1,172]{0,1,3,2:T(8,128)(2,1)}, u32[]{:S(2)}, u32[]{:S(2)}) collective-permute-start(bf16[512,8,1,172]{0,1,3,2:T(8,128)(2,1)} %bitcast.279), channel_id=1, source_target_pairs={{0,3},{1,2},{2,1},{3,0},{4,7},{5,6},{6,5},{7,4},{8,11},{9,10},{10,... | collective-permute-start | bytes 4227080 | tf_op jit(solution)/shard_map/ppermute | solution.py:30
  2076.2 301.3 %all-to-all-start.12 = ((bf16[512,8,4,172]{0,1,3,2:T(8,128)(2,1)}), bf16[512,8,4,172]{0,1,3,2:T(8,128)(2,1)}, u32[]{:S(2)}, u32[]{:S(2)}) async-start(bf16[512,8,4,172]{0,1,3,2:T(8,128)(2,1)} %copy.189), calls=%async_computation.12 | async-start | bytes 11272192 | tf_op jit(solution)/shard_map/all_to_all | solution.py:310
  2081.4 383.6 %all-gather.26.cloned.1.call-start = ((), (), s32[]{:S(2)}) async-start(), calls=%async_computation.17 | async-start | bytes 10485760 | tf_op jit(solution)/shard_map/all_gather | solution.py:317
  2647.7 259.0 %copy-start.22 = (f32[512]{0:T(512)S(1)}, f32[512]{0:T(512)}, u32[]{:S(2)}) copy-start(f32[512]{0:T(512)} %copy-done.20) | copy-start | bytes 6148
  2647.7 259.0 %copy-start.29 = (f32[512]{0:T(512)S(1)}, f32[512]{0:T(512)}, u32[]{:S(2)}) copy-start(f32[512]{0:T(512)} %copy-done.28) | copy-start | bytes 6148
  2902.3 12.4 collective-permute-start.3
  (42 other events, 954.8 us)
Sparse Core Ops, SparseCore 0:
  11.0 80.1 all-gather.17
  94.0 101.4 all-gather.19
  198.5 109.8 all-gather.21
  311.2 108.5 all-gather.23
  422.5 161.4 all-gather.37
  586.7 153.4 all-gather.39
  743.0 142.7 all-gather.41
  887.4 164.3 all-gather.33
  1053.4 206.5 all-gather.35
  1261.4 147.7 all-gather.31
  1498.9 271.1 all-gather.27
  1820.0 349.5 all-gather.29
  2253.2 211.6 all-gather.25
